TPU v7x, 128 devices: a whole 4x4x4 slice. The times are simulated.
128 devices in a mesh: seq: 32 (over y, x, core), head: 4 (over z).
Axes of the slice: x: 4, y: 4, z: 4, core: 2. Of those that a mesh axis runs over, the one named last changes fastest.
Arguments:
- hidden_in: bfloat16 [8192, 2880], P(('seq', 'head')), may hold values from -16 to 16
- qkv_new: bfloat16 [8192, 8, 640], P(('seq', 'head')), may hold values from -250 to 250
- kv_cache: bfloat16 [32, 8192, 8, 128], P('seq', None, 'head'), may hold values from -4 to 4
- cache_len: int32 [32], P('seq'), may hold values from 2048 to 8192, as said below
- o_weight: bfloat16 [4096, 2880], P('head'), may hold values from -1 to 1
- norm_gain: float32 [2880], replicated, may hold values from 0.1 to 1.9
- expert_ids: int32 [8192, 4], P(('seq', 'head')), may hold values from 0 to 31, all different within a row; in each aligned block of 64 rows (0 to 63, 64 to 127, ...) at most 10 rows name the same one
- gate_weights: float32 [8192, 4], P(('seq', 'head')), may hold values from 0.1 to 1
- w_gate_up: bfloat16 [32, 2880, 2, 2880], P('seq', None, None, 'head'), may hold values from -0.109375 to 0.109375
- w_down: bfloat16 [32, 2880, 2880], P('seq', 'head'), may hold values from -0.109375 to 0.109375
Outputs:
- attn_proj: bfloat16 [8192, 2880], P(('seq', 'head'))
- moe_out: bfloat16 [8192, 2880], P(('seq', 'head'))
Inputs may be any that keep to these rules, and one draw needn't show every extreme that they name: `cache_len`: some sequence has exactly 8192 live cached positions in every draw. `expert_ids`: each token names 4 different experts. Among the tokens of one device (aligned blocks of 64 tokens) no expert is named more than 10 times, a bound that some block reaches.
All inputs are finite; a program needn't handle non-finite values.
Results may differ from a plain program's by a relative error of at most 0.024.
Values may be sent and summed in bfloat16 or wider, within the bound.
A program may use at most 256 MiB of HBM per device.

v0:
```python
import jax
import jax.numpy as jnp
from jax import lax
from jax.sharding import PartitionSpec as P

TOP = 4


epsilon = 1e-05


def attend(fresh_group, stored, live_len):
    fresh_len = fresh_group.shape[0]
    cached = stored.shape[0]
    head_dim = stored.shape[1] // 2
    group_size = fresh_group.shape[1] // head_dim - 2
    queries = fresh_group[:, : group_size * head_dim].reshape(fresh_len * group_size, head_dim)
    key_rows = jnp.concatenate(
        [stored[:, :head_dim], fresh_group[:, group_size * head_dim : (group_size + 1) * head_dim]],
        axis=0,
    )
    value_rows = jnp.concatenate(
        [stored[:, head_dim:], fresh_group[:, (group_size + 1) * head_dim :]], axis=0
    )
    scores = jnp.einsum(
        "qd,kd->qk", queries, key_rows, preferred_element_type=jnp.float32
    ) * head_dim ** (-0.5)
    positions = lax.broadcasted_iota(jnp.int32, scores.shape, 1)
    token_pos = lax.broadcasted_iota(jnp.int32, scores.shape, 0) // group_size
    visible = (positions < live_len) | (positions >= cached) & (positions - cached <= token_pos)
    masked = jnp.where(visible, scores, -jnp.inf)
    row_max = jnp.max(masked, axis=1, keepdims=True)
    exponent = jnp.where(visible, jnp.exp(masked - row_max), 0.0)
    weights = (exponent / jnp.sum(exponent, axis=1, keepdims=True)).astype(jnp.bfloat16)
    result = jnp.dot(weights, value_rows, preferred_element_type=jnp.float32).astype(jnp.bfloat16)
    return result.reshape(fresh_len, group_size * head_dim)


def expert_rows(slot_rows, w_gate_up, w_down):
    local_count = w_gate_up.shape[0]
    part_width = w_gate_up.shape[3]
    merged = w_gate_up.reshape(local_count, w_gate_up.shape[1], 2 * part_width)
    gate_up = jnp.einsum("sxcd,xdf->sxcf", slot_rows, merged, preferred_element_type=jnp.float32)
    hidden = (jax.nn.silu(gate_up[..., :part_width]) * gate_up[..., part_width:]).astype(
        jnp.bfloat16
    )
    return jnp.einsum("sxcf,xfd->sxcd", hidden, w_down, preferred_element_type=jnp.float32)


def per_device(
    hidden_in,
    qkv_new,
    kv_cache,
    cache_len,
    o_weight,
    norm_gain,
    expert_ids,
    gate_weights,
    w_gate_up,
    w_down,
):
    seq_count = lax.axis_size("seq")
    head_count = lax.axis_size("head")
    tok_rows = hidden_in.shape[0]
    model_width = hidden_in.shape[1]
    local_count = w_gate_up.shape[0]
    experts = local_count * seq_count
    capacity = max(2, tok_rows * TOP * 5 // (4 * experts))
    fresh_rows = lax.all_to_all(qkv_new, "head", split_axis=1, concat_axis=0, tiled=True)
    kv_local = fresh_rows.shape[1]
    live_len = cache_len[0]
    stored_all = kv_cache[0]

    def one_head(head_index):
        fresh_group = lax.dynamic_index_in_dim(fresh_rows, head_index, 1, keepdims=False)
        stored = lax.dynamic_index_in_dim(stored_all, head_index, 1, keepdims=False)
        return attend(fresh_group, stored, live_len)

    attended = lax.map(one_head, jnp.arange(kv_local, dtype=jnp.int32))
    attention = jnp.moveaxis(attended, 0, 1).reshape(fresh_rows.shape[0], -1)
    projected = lax.psum_scatter(
        jnp.dot(attention, o_weight, preferred_element_type=jnp.float32),
        "head",
        scatter_dimension=0,
        tiled=True,
    )
    attn_proj = projected.astype(jnp.bfloat16)
    kept_proj = lax.optimization_barrier(attn_proj)
    residual = (hidden_in.astype(jnp.float32) + kept_proj.astype(jnp.float32)).astype(jnp.bfloat16)
    widened = lax.optimization_barrier(residual).astype(jnp.float32)
    normed = (
        widened
        * lax.rsqrt(jnp.mean(widened * widened, axis=1, keepdims=True) + epsilon)
        * norm_gain
    ).astype(jnp.bfloat16)
    flat_ids = expert_ids.reshape(-1)
    onehot = (flat_ids[:, None] == jnp.arange(experts, dtype=jnp.int32)[None, :]).astype(jnp.int32)
    before = jnp.cumsum(onehot, axis=0) - onehot
    slot_ids = jnp.sum(before * onehot, axis=1)
    target = flat_ids * capacity + slot_ids
    places = target[None, :] == jnp.arange(experts * capacity, dtype=jnp.int32)[:, None]
    places = jnp.any(places.reshape(experts * capacity, tok_rows, TOP), axis=2).astype(jnp.bfloat16)
    outgoing = jnp.dot(places, normed, preferred_element_type=jnp.float32).astype(jnp.bfloat16)
    outgoing = outgoing.reshape(seq_count, local_count, capacity, model_width)
    copies = jnp.broadcast_to(
        outgoing[:, None], (seq_count, head_count, local_count, capacity, model_width)
    )
    copies = copies.reshape(seq_count * head_count, local_count, capacity, model_width)
    partial_value = expert_rows(
        lax.all_to_all(copies, ("seq", "head"), split_axis=0, concat_axis=0, tiled=True),
        w_gate_up,
        w_down,
    ).astype(jnp.bfloat16)
    returned = lax.all_to_all(
        partial_value, ("seq", "head"), split_axis=0, concat_axis=0, tiled=True
    )
    returned = returned.reshape(seq_count, head_count, local_count, capacity, model_width)
    expert_back = jnp.sum(returned.astype(jnp.float32), axis=1).astype(jnp.bfloat16)
    flat_out = expert_back.reshape(experts * capacity, model_width)
    picked = (
        jnp.take(flat_out, target, axis=0).reshape(tok_rows, TOP, model_width).astype(jnp.float32)
    )
    moe_out = jnp.sum(picked * gate_weights[:, :, None], axis=1).astype(jnp.bfloat16)
    return (attn_proj, moe_out)


def solution(mesh):
    return jax.shard_map(
        per_device,
        mesh=mesh,
        in_specs=(
            P(("seq", "head"), None),
            P(("seq", "head"), None, None),
            P("seq", None, "head", None),
            P("seq"),
            P("head", None),
            P(),
            P(("seq", "head"), None),
            P(("seq", "head"), None),
            P("seq", None, None, "head"),
            P("seq", "head", None),
        ),
        out_specs=(P(("seq", "head"), None), P(("seq", "head"), None)),
        check_vma=False,
    )
```

profile of v0, /device:TPU:3, one launch (start us, length us, event | category | flops | bytes accessed | tf_op | source)
XLA Modules:
  0.0 694.1 jit_solution(7500185220060461084)
XLA Ops:
  9.2 5.0 all-to-all-start
  14.2 4.8 copy.90
  19.0 5.2 all-to-all-done
  25.6 221.4 %while.12 = (s32[]{:T(128)}, bf16[2,256,512]{1,2,0:T(8,128)(2,1)}, s32[]{:T(128)}, s32[2]{0:T(128)}, bf16[256,2,640]{2,0,1:T(8,128)(2,1)}, /*index=5*/bf16[8192,...) while((s32[]{:T(128)}, bf16[2,256,512]{1,2,0:T(8,128)(2,1)}, s32[]{:T(128)}, s32[2]{0:T(128)}, ...), condition=%wide.region_3.4_spmd, body=%wide.region_0.3_spmd.sunk | while | flops 4883516416 | bytes 227137744 | solution.py:79
  33.6 28.3 %fusion.69 = (f32[2048]{0:T(1024)S(1)}, f32[2048,8448]{1,0:T(8,128)}) fusion(s32[2048]{0:T(1024)S(1)} %get-tuple-element.153, s32[2048]{0:T(1024)S(1)} %get-tuple-element.154, pred[2048]{0:T(1024)(128)(4,1)S(1)} %fusion.66, s32[8448]{0:T(1024)S(1)} %iota_add_fusion.2, pred[8448]{0:T(1024)(128)(4,1)S(1)} %get-tuple-element.155, ...), kind=kOutput, calls=%fused_computation.7.clone.1 | convolution fusion | flops 2337863680 | bytes 70626816 | tf_op jit(solution)/shard_map/while/body/eval_jaxpr/qd,kd->qk/dot_general | solution.py:25
  61.9 35.6 %fusion.70 = f32[2048]{0:T(1024)S(1)} fusion(f32[2048,8448]{1,0:T(8,128)} %get-tuple-element.159, f32[2048]{0:T(1024)S(1)} %get-tuple-element.160, s32[2048]{0:T(1024)S(1)} %get-tuple-element.153, s32[2048]{0:T(1024)S(1)} %get-tuple-element.154, pred[2048]{0:T(1024)(128)(4,1)S(1)} %fusion.66, s32[8448]{0:T(1024)S(1)} %iota_add_fusion.2, ...), kind=kLoop, calls=%fused_computation.8.clone.1 | loop fusion | flops 155711488 | bytes 69291520 | tf_op jit(solution)/shard_map/while/body/eval_jaxpr/reduce_sum | solution.py:34
  97.5 37.0 %fusion.71 = bf16[2048,64]{0,1:T(8,128)(2,1)S(1)} fusion(f32[2048,8448]{1,0:T(8,128)} %get-tuple-element.159, f32[2048]{0:T(1024)S(1)} %fusion.70, f32[2048]{0:T(1024)S(1)} %get-tuple-element.160, bf16[256,64]{1,0:T(8,128)(2,1)S(1)} %get-tuple-element.161, bf16[8192,64]{1,0:T(8,128)(2,1)S(1)} %get-tuple-element.162, ...), kind=kOutput, calls=%fused_computation.10.clone.3 | convolution fusion | flops 2389901312 | bytes 70635008 | tf_op jit(solution)/shard_map/while/body/eval_jaxpr/dot_general | solution.py:35
  144.1 28.3 %fusion.69 = (f32[2048]{0:T(1024)S(1)}, f32[2048,8448]{1,0:T(8,128)}) fusion(s32[2048]{0:T(1024)S(1)} %get-tuple-element.153, s32[2048]{0:T(1024)S(1)} %get-tuple-element.154, pred[2048]{0:T(1024)(128)(4,1)S(1)} %fusion.66, s32[8448]{0:T(1024)S(1)} %iota_add_fusion.2, pred[8448]{0:T(1024)(128)(4,1)S(1)} %get-tuple-element.155, ...), kind=kOutput, calls=%fused_computation.7.clone.1 | convolution fusion | flops 2337863680 | bytes 70626816 | tf_op jit(solution)/shard_map/while/body/eval_jaxpr/qd,kd->qk/dot_general | solution.py:25
  172.4 35.6 %fusion.70 = f32[2048]{0:T(1024)S(1)} fusion(f32[2048,8448]{1,0:T(8,128)} %get-tuple-element.159, f32[2048]{0:T(1024)S(1)} %get-tuple-element.160, s32[2048]{0:T(1024)S(1)} %get-tuple-element.153, s32[2048]{0:T(1024)S(1)} %get-tuple-element.154, pred[2048]{0:T(1024)(128)(4,1)S(1)} %fusion.66, s32[8448]{0:T(1024)S(1)} %iota_add_fusion.2, ...), kind=kLoop, calls=%fused_computation.8.clone.1 | loop fusion | flops 155711488 | bytes 69291520 | tf_op jit(solution)/shard_map/while/body/eval_jaxpr/reduce_sum | solution.py:34
  208.0 37.0 %fusion.71 = bf16[2048,64]{0,1:T(8,128)(2,1)S(1)} fusion(f32[2048,8448]{1,0:T(8,128)} %get-tuple-element.159, f32[2048]{0:T(1024)S(1)} %fusion.70, f32[2048]{0:T(1024)S(1)} %get-tuple-element.160, bf16[256,64]{1,0:T(8,128)(2,1)S(1)} %get-tuple-element.161, bf16[8192,64]{1,0:T(8,128)(2,1)S(1)} %get-tuple-element.162, ...), kind=kOutput, calls=%fused_computation.10.clone.3 | convolution fusion | flops 2389901312 | bytes 70635008 | tf_op jit(solution)/shard_map/while/body/eval_jaxpr/dot_general | solution.py:35
  247.0 6.4 fusion.47
  255.0 36.5 %reduce-scatter.2.cloned.1.call-done = f32[64,2880]{1,0:T(8,128)} async-done(((f32[256,2880]{1,0:T(8,128)}), f32[64,2880]{1,0:T(8,128)}) %reduce-scatter.2.cloned.1.call-update) | async-done | bytes 737296 | tf_op jit(solution)/shard_map/reduce_scatter | solution.py:81
  295.7 2.7 broadcast_in_dim.52
  298.4 5.2 broadcast_in_dim.53.clone
  303.6 145.0 %all_to_all.28 = bf16[128,1,10,2880]{3,2,1,0:T(8,128)(2,1)} all-to-all(bf16[128,1,10,2880]{3,2,1,0:T(8,128)(2,1)} %bitcast.82), channel_id=1, replica_groups=mesh['seq'=32,'head'=4] {'seq','head'}, dimensions={0} | all-to-all | bytes 14745600 | tf_op jit(solution)/shard_map/all_to_all | solution.py:110
  448.6 15.8 %copy.74 = bf16[128,1,10,2880]{0,3,2,1:T(8,128)(2,1)} copy(bf16[128,1,10,2880]{3,2,1,0:T(8,128)(2,1)} %all_to_all.28) | data formatting | bytes 14745600 | tf_op jit(solution)/shard_map/all_to_all | solution.py:110
  464.4 17.5 %fusion.24 = f32[128,1,10,1440]{0,3,2,1:T(8,128)} fusion(bf16[2880,1440,1]{0,1,2:T(8,128)(2,1)} %bitcast.86, bf16[128,1,10,2880]{0,3,2,1:T(8,128)(2,1)} %copy.74), kind=kOutput, calls=%fused_computation.40 | convolution fusion | flops 10616832000 | bytes 23040000 | tf_op jit(solution)/shard_map/sxcd,xdf->sxcf/dot_general | solution.py:43
  481.9 11.8 %convert_bitcast_fusion = bf16[128,1,10,2880]{0,3,2,1:T(8,128)(2,1)} fusion(bf16[1,720,2880]{2,1,0:T(8,128)(2,1)S(1)} %bitcast.88, f32[128,1,10,1440]{0,3,2,1:T(8,128)} %fusion.24), kind=kOutput, calls=%fused_computation.39 | convolution fusion | flops 5317632000 | bytes 18892800 | tf_op jit(solution)/shard_map/sxcf,xfd->sxcd/dot_general | solution.py:47
  493.7 15.6 %copy.75 = bf16[128,1,10,2880]{3,2,1,0:T(8,128)(2,1)} copy(bf16[128,1,10,2880]{0,3,2,1:T(8,128)(2,1)} %convert_bitcast_fusion) | data formatting | bytes 14745600 | tf_op jit(solution)/shard_map/convert_element_type | solution.py:113
  509.3 7.2 %all-to-all-start.2 = ((bf16[128,1,10,2880]{3,2,1,0:T(8,128)(2,1)}), bf16[128,1,10,2880]{3,2,1,0:T(8,128)(2,1)}, u32[]{:S(2)}, u32[]{:S(2)}) async-start(bf16[128,1,10,2880]{3,2,1,0:T(8,128)(2,1)} %copy.75), calls=%async_computation.3 | async-start | bytes 24117248 | tf_op jit(solution)/shard_map/all_to_all | solution.py:114
  517.0 152.0 %all-to-all-done.2 = bf16[128,1,10,2880]{3,2,1,0:T(8,128)(2,1)} async-done(((bf16[128,1,10,2880]{3,2,1,0:T(8,128)(2,1)}), bf16[128,1,10,2880]{3,2,1,0:T(8,128)(2,1)}, u32[]{:S(2)}, u32[]{:S(2)}) %all-to-all-start.2) | async-done | bytes 7372832 | tf_op jit(solution)/shard_map/all_to_all | solution.py:114
  668.9 9.2 %bitcast_reduce_fusion = bf16[32,10,2880]{2,1,0:T(8,128)(2,1)} fusion(bf16[32,4,10,2880]{3,2,1,0:T(8,128)(2,1)} %bitcast.72), kind=kLoop, calls=%fused_computation.36 | loop fusion | flops 2764800 | bytes 9216000 | tf_op jit(solution)/shard_map/reduce_sum | solution.py:118
  678.1 3.2 reshape.146
  683.3 3.7 multiply_reduce_fusion
  (86 shorter events, 26.5 us)
Async XLA Ops:
  9.2 15.1 %all-to-all-start = ((bf16[64,8,640]{2,0,1:T(8,128)(2,1)}), bf16[64,8,640]{2,0,1:T(8,128)(2,1)S(1)}, u32[]{:S(2)}, u32[]{:S(2)}) async-start(bf16[64,8,640]{2,0,1:T(8,128)(2,1)} %copy.63), calls=%async_computation | async-start | bytes 1310720 | tf_op jit(solution)/shard_map/all_to_all | solution.py:69
  14.2 277.3 %reduce-scatter.2.cloned.1.call-start = ((), (), s32[]{:S(2)}) async-start(), calls=%async_computation.4 | async-start | bytes 3768320 | tf_op jit(solution)/shard_map/reduce_scatter | solution.py:81
  97.5 37.8 %copy-start.5 = (bf16[2,256,512]{1,2,0:T(8,128)(2,1)S(1)}, bf16[2,256,512]{1,2,0:T(8,128)(2,1)}, u32[]{:S(2)}) copy-start(bf16[2,256,512]{1,2,0:T(8,128)(2,1)} %get-tuple-element.173) | copy-start | bytes 1572868 | tf_op jit(solution)/shard_map/while
  135.3 0.8 copy-start.6
  208.0 37.8 %copy-start.5 = (bf16[2,256,512]{1,2,0:T(8,128)(2,1)S(1)}, bf16[2,256,512]{1,2,0:T(8,128)(2,1)}, u32[]{:S(2)}) copy-start(bf16[2,256,512]{1,2,0:T(8,128)(2,1)} %get-tuple-element.173) | copy-start | bytes 1572868 | tf_op jit(solution)/shard_map/while
  245.8 0.8 copy-start.6
  247.0 6.4 copy-start.2
  247.0 46.4 %copy-start.1 = (bf16[64,2880]{1,0:T(8,128)(2,1)S(1)}, bf16[64,2880]{1,0:T(8,128)(2,1)}, u32[]{:S(2)}) copy-start(bf16[64,2880]{1,0:T(8,128)(2,1)} %param.12) | copy-start | bytes 1105924
  247.0 46.7 %copy-start.3 = (f32[2880]{0:T(1024)S(1)}, f32[2880]{0:T(1024)}, u32[]{:S(2)}) copy-start(f32[2880]{0:T(1024)} %param.17) | copy-start | bytes 34564
  292.7 0.7 copy-start
  448.6 33.3 %slice-start = ((s8[4239360]{0:T(1024)(128)(4,1)}), s8[45056]{0:T(1024)(128)(4,1)S(1)}, s32[]{:S(2)}) async-start(s8[4239360]{0:T(1024)(128)(4,1)} %bitcast.87), calls=%async_computation.5 | async-start | bytes 90112
  464.4 17.5 %slice-start.1 = ((s8[4239360]{0:T(1024)(128)(4,1)}), s8[4194304]{0:T(1024)(128)(4,1)S(1)}, s32[]{:S(2)}) async-start(s8[4239360]{0:T(1024)(128)(4,1)} %bitcast.87), calls=%async_computation.6 | async-start | bytes 8388608
  509.3 7.2 %copy-start.4 = (f32[64,4]{0,1:T(4,128)S(1)}, f32[64,4]{0,1:T(4,128)}, u32[]{:S(2)}) copy-start(f32[64,4]{0,1:T(4,128)} %param.19) | copy-start | bytes 3076
  509.3 159.6 %all-to-all-start.2 = ((bf16[128,1,10,2880]{3,2,1,0:T(8,128)(2,1)}), bf16[128,1,10,2880]{3,2,1,0:T(8,128)(2,1)}, u32[]{:S(2)}, u32[]{:S(2)}) async-start(bf16[128,1,10,2880]{3,2,1,0:T(8,128)(2,1)} %copy.75), calls=%async_computation.3 | async-start | bytes 24117248 | tf_op jit(solution)/shard_map/all_to_all | solution.py:114
Sparse Core Ops, SparseCore 0:
  253.5 37.9 reduce-scatter.1
where the time goes:
time: 706 us; the launch traced here: 694 us
  waiting for transfers between devices  194 us (27%)
  matrix products  168 us (24%)
  blocking collectives  145 us (21%)
  other arithmetic  87.8 us (12%)
  local copies, waits for them, and re-layouts  67.9 us (10%)
  between operations  14.4 us (2%)
  starting transfers between devices  12.2 us (2%)
    all_to_all x1, waiting for transfers between devices, per_device(): lax.all_to_all(partial_value, ('seq', 'head'), split_axis=0, concat_axis=...  152 us
    all_to_all x1, blocking collectives, per_device(): lax.all_to_all(copies, ('seq', 'head'), split_axis=0, concat_axis=0, tile...  145 us
    dot_general x2, matrix products, attend(): jnp.dot(weights, value_rows, preferred_element_type=jnp.float32)  74 us
    reduce_sum x2, other arithmetic, attend(): jnp.sum(exponent, axis=1, keepdims=True)  71.2 us
    dot_general x2, matrix products, attend(): jnp.einsum('qd,kd->qk', queries, key_rows, preferred_element_type=jnp.flo...  56.6 us
    reduce_scatter x1, waiting for transfers between devices, per_device(): lax.psum_scatter(jnp.dot(attention, o_weight, preferred_element_type=jnp....  36.5 us
    dot_general x1, matrix products, expert_rows(): jnp.einsum('sxcd,xdf->sxcf', slot_rows, merged, preferred_element_type=jn...  17.5 us
    all_to_all x1, local copies, waits for them, and re-layouts, per_device(): lax.all_to_all(copies, ('seq', 'head'), split_axis=0, concat_axis=0, tile...  15.8 us
  transfers between devices with their start and end apart: 3, of which 3 were waited for; matrix products, arithmetic and copies ran while one was open for 1% of the time, Pallas kernels for 0%

commit v1 on v0

v1 whole, which is shorter than its diff:
```python
import functools
import jax
import jax.numpy as jnp
from jax import lax
from jax.experimental import pallas as pl
from jax.experimental.pallas import tpu as pltpu
from jax.sharding import PartitionSpec as P

TOP = 4
EPS = 1e-05
LOG2E = 1.4426950408889634
MASKED = -1e30
NT = (((1,), (1,)), ((), ()))


def attend_kernel(len_ref, new_ref, kk_ref, vv_ref, out_ref, q_s, nk_s, nv_s, s_s, acc_s, *, tile):
    src_count, _, tok, width = new_ref.shape
    cached = kk_ref.shape[1]
    head_dim = kk_ref.shape[2] // 2
    group = width // head_dim - 2
    rows = group * tok
    new_len = src_count * tok
    chunk = pl.program_id(1)
    live = len_ref[0]
    factor = LOG2E * head_dim ** (-0.5)
    for r in range(group):
        wide = new_ref[chunk, 0, :, r * head_dim : (r + 1) * head_dim].astype(jnp.float32) * factor
        high = wide.astype(jnp.bfloat16)
        low = (wide - high.astype(jnp.float32)).astype(jnp.bfloat16)
        q_s[r * tok : (r + 1) * tok, :] = jnp.concatenate([high, low], axis=1)
    for s in range(src_count):
        k = new_ref[s, 0, :, group * head_dim : (group + 1) * head_dim]
        v = new_ref[s, 0, :, (group + 1) * head_dim :]
        nk_s[s * tok : (s + 1) * tok, :] = jnp.concatenate([k, k], axis=1)
        nv_s[s * tok : (s + 1) * tok, :] = jnp.concatenate([jnp.ones_like(v), v], axis=1)
    tiles = rows // tile

    def scores(i, slot):
        start = pl.multiple_of(i * tile, tile)
        q = q_s[pl.ds(start, tile), :]
        s_s[slot, :, :cached] = lax.dot_general(
            q, kk_ref[0], NT, preferred_element_type=jnp.float32
        )
        fresh = lax.dot_general(q, nk_s[...], NT, preferred_element_type=jnp.float32)
        key_pos = lax.broadcasted_iota(jnp.int32, (tile, new_len), 1)
        tok_pos = chunk * tok + (lax.broadcasted_iota(jnp.int32, (tile, new_len), 0) + start) % tok
        s_s[slot, :, cached:] = jnp.where(key_pos <= tok_pos, fresh, MASKED)

        def hide(c, carry):
            at = pl.multiple_of(c * 128, 128)
            pos = at + lax.broadcasted_iota(jnp.int32, (tile, 128), 1)
            s_s[slot, :, pl.ds(at, 128)] = jnp.where(
                pos < live, s_s[slot, :, pl.ds(at, 128)], MASKED
            )
            return carry

        lax.fori_loop(live // 128, cached // 128, hide, 0)

    def weigh(i, slot):
        start = pl.multiple_of(i * tile, tile)
        s = s_s[slot]
        p = jnp.exp2(s - jnp.max(s, axis=1, keepdims=True)).astype(jnp.bfloat16)
        acc_s[pl.ds(start, tile), :] = jnp.dot(
            p[:, :cached], vv_ref[0], preferred_element_type=jnp.float32
        ) + jnp.dot(p[:, cached:], nv_s[...], preferred_element_type=jnp.float32)

    scores(0, 0)

    def pair(u, carry):
        scores(2 * u + 1, 1)
        weigh(2 * u, 0)
        scores(lax.rem(2 * u + 2, tiles), 0)
        weigh(2 * u + 1, 1)
        return carry

    lax.fori_loop(0, tiles // 2, pair, 0)
    for r in range(group):
        acc = acc_s[r * tok : (r + 1) * tok, :]
        out_ref[:, r * head_dim : (r + 1) * head_dim] = (
            acc[:, head_dim:] / acc[:, :head_dim]
        ).astype(jnp.bfloat16)


def attention_of(fresh, kk, vv, live, tile=256):
    src_count, kv_local, tok, width = fresh.shape
    cached, lanes = kk.shape[1:]
    group = width * 2 // lanes - 2
    rows = group * tok
    return pl.pallas_call(
        functools.partial(attend_kernel, tile=tile),
        grid_spec=pltpu.PrefetchScalarGridSpec(
            num_scalar_prefetch=1,
            grid=(kv_local, src_count),
            in_specs=[
                pl.BlockSpec((src_count, 1, tok, width), lambda h, j, n: (0, h, 0, 0)),
                pl.BlockSpec((1, cached, lanes), lambda h, j, n: (h, 0, 0)),
                pl.BlockSpec((1, cached, lanes), lambda h, j, n: (h, 0, 0)),
            ],
            out_specs=pl.BlockSpec((tok, group * lanes // 2), lambda h, j, n: (j, h)),
            scratch_shapes=[
                pltpu.VMEM((rows, lanes), jnp.bfloat16),
                pltpu.VMEM((src_count * tok, lanes), jnp.bfloat16),
                pltpu.VMEM((src_count * tok, lanes), jnp.bfloat16),
                pltpu.VMEM((2, tile, cached + src_count * tok), jnp.float32),
                pltpu.VMEM((rows, lanes), jnp.float32),
            ],
        ),
        out_shape=jax.ShapeDtypeStruct(
            (src_count * tok, kv_local * group * lanes // 2), jnp.bfloat16
        ),
        compiler_params=pltpu.CompilerParams(vmem_limit_bytes=56 << 20),
    )(live, fresh, kk, vv)


def per_device(
    hidden_in,
    qkv_new,
    kv_cache,
    cache_len,
    o_weight,
    norm_gain,
    expert_ids,
    gate_weights,
    w_gate_up,
    w_down,
):
    seq_count = lax.axis_size("seq")
    head_count = lax.axis_size("head")
    tok_rows, model_width = hidden_in.shape
    experts = seq_count
    capacity = max(2, tok_rows * TOP * 5 // (4 * experts))
    half = w_gate_up.shape[3]
    head_dim = kv_cache.shape[3] // 2

    fresh = lax.all_to_all(
        jnp.transpose(qkv_new, (1, 0, 2)), "head", split_axis=0, concat_axis=0, tiled=True
    )
    fresh = fresh.reshape(head_count, -1, tok_rows, qkv_new.shape[2])
    stored = jnp.transpose(kv_cache[0], (1, 0, 2))
    k, v = stored[..., :head_dim], stored[..., head_dim:]
    kk = jnp.concatenate([k, k], axis=-1)
    vv = jnp.concatenate([jnp.ones_like(v), v], axis=-1)
    attention = attention_of(fresh, kk, vv, cache_len)
    projected = lax.psum_scatter(
        jnp.dot(attention, o_weight, preferred_element_type=jnp.float32).astype(jnp.bfloat16),
        "head",
        scatter_dimension=0,
        tiled=True,
    )
    attn_proj = projected.astype(jnp.bfloat16)
    widened = (
        (hidden_in.astype(jnp.float32) + attn_proj.astype(jnp.float32))
        .astype(jnp.bfloat16)
        .astype(jnp.float32)
    )
    normed = (
        widened
        * lax.rsqrt(jnp.mean(widened * widened, axis=1, keepdims=True) + EPS)
        * norm_gain
    ).astype(jnp.bfloat16)

    flat_ids = expert_ids.reshape(-1)
    onehot = (flat_ids[:, None] == jnp.arange(experts, dtype=jnp.int32)[None, :]).astype(jnp.int32)
    before = jnp.cumsum(onehot, axis=0) - onehot
    slot_ids = jnp.sum(before * onehot, axis=1)
    target = flat_ids * capacity + slot_ids
    places = target[None, :] == jnp.arange(experts * capacity, dtype=jnp.int32)[:, None]
    places = places.reshape(experts * capacity, tok_rows, TOP)
    gates = jnp.sum(jnp.where(places, gate_weights[None], 0.0), axis=2).T
    gates_high = gates.astype(jnp.bfloat16)
    gates_low = (gates - gates_high.astype(jnp.float32)).astype(jnp.bfloat16)
    gates = jnp.concatenate([gates_high, gates_low], axis=0)
    places = jnp.any(places, axis=2).astype(jnp.bfloat16)

    outgoing = jnp.dot(places, normed, preferred_element_type=jnp.float32).astype(jnp.bfloat16)
    outgoing = outgoing.reshape(experts, capacity, model_width)
    arrived = lax.all_to_all(outgoing, "seq", split_axis=0, concat_axis=0, tiled=True)
    rows = lax.all_gather(
        arrived.reshape(experts * capacity, model_width), "head", axis=0, tiled=True
    )
    gate_up = jnp.dot(
        rows,
        w_gate_up[0].reshape(model_width, 2 * half),
        preferred_element_type=jnp.float32,
    )
    hidden = (jax.nn.silu(gate_up[:, :half]) * gate_up[:, half:]).astype(jnp.bfloat16)
    piece = jnp.dot(hidden, w_down[0], preferred_element_type=jnp.float32).astype(jnp.bfloat16)
    summed = lax.psum_scatter(piece, "head", scatter_dimension=0, tiled=True)
    returned = lax.all_to_all(
        summed.reshape(experts, capacity, model_width), "seq", split_axis=0, concat_axis=0, tiled=True
    ).reshape(experts * capacity, model_width)
    both = jnp.dot(gates, returned, preferred_element_type=jnp.float32)
    moe_out = (both[:tok_rows] + both[tok_rows:]).astype(jnp.bfloat16)
    return (attn_proj, moe_out)


def solution(mesh):
    return jax.shard_map(
        per_device,
        mesh=mesh,
        in_specs=(
            P(("seq", "head"), None),
            P(("seq", "head"), None, None),
            P("seq", None, "head", None),
            P("seq"),
            P("head", None),
            P(),
            P(("seq", "head"), None),
            P(("seq", "head"), None),
            P("seq", None, None, "head"),
            P("seq", "head", None),
        ),
        out_specs=(P(("seq", "head"), None), P(("seq", "head"), None)),
        check_vma=False,
    )
```

time: 706 us -> 434 us (0.61); the launches traced: 694 us -> 431 us
  matrix products: 168 us -> 36.3 us
  blocking collectives: 145 us -> 46.1 us
  other arithmetic: 87.8 us -> 6.32 us
  Pallas kernels: 0 us -> 61.5 us
  local copies, waits for them, and re-layouts: 67.9 us -> 26 us
  waiting for transfers between devices: 194 us -> 227 us
    dot_general x6 -> x3, matrix products: 160 us -> 27.4 us  [the longest x1 16.4 us: per_device(): jnp.dot(rows, w_gate_up[0].reshape(model_width, 2 * half), preferred_elem...]
    all_to_all x2, waiting for transfers between devices: 157 us -> 37.4 us  [the longest x1 37.4 us: per_device(): lax.all_to_all(summed.reshape(experts, capacity, model_width), 'seq', spl...]
    all_to_all x1, blocking collectives: 145 us -> 46.1 us  [per_device(): lax.all_to_all(outgoing, 'seq', split_axis=0, concat_axis=0, tiled=True)]
    reduce_sum x5 -> x2, other arithmetic: 84.3 us -> 1.35 us  [the longest x1 1.21 us: per_device(): jnp.mean(widened * widened, axis=1, keepdims=True) + EPS]
    reduce_scatter x0 -> x1, waiting for transfers between devices: none -> 75.3 us  [per_device(): summed = lax.psum_scatter(piece, 'head', scatter_dimension=0, tiled=True)]
    all_gather x0 -> x1, waiting for transfers between devices: none -> 72.7 us  [per_device(): lax.all_gather(arrived.reshape(experts * capacity, model_width), 'head',...]
    pallas_call x0 -> x1, Pallas kernels: none -> 61.5 us  [attention_of(): pl.pallas_call(functools.partial(attend_kernel, tile=tile), grid_spec=plt...]
    all_to_all x2 -> x0, local copies, waits for them, and re-layouts: 16.7 us -> none  [the longest x1 15.8 us: per_device(): lax.all_to_all(copies, ('seq', 'head'), split_axis=0, concat_axis=0, tile...]
  transfers between devices with their start and end apart: 3 -> 5, of which waited for: 3 -> 4; matrix products, arithmetic and copies ran while one was open for 1% -> 3% of each run, Pallas kernels for 0% -> 0%
where the time goes in v1:
time: 434 us; the launch traced here: 431 us
  waiting for transfers between devices  227 us (52%)
  Pallas kernels  61.5 us (14%)
  blocking collectives  46.1 us (11%)
  matrix products  36.3 us (8%)
  local copies, waits for them, and re-layouts  26 us (6%)
  between operations  14.6 us (3%)
  starting transfers between devices  13 us (3%)
  other arithmetic  6.32 us (1%)
    reduce_scatter x1, waiting for transfers between devices, per_device(): summed = lax.psum_scatter(piece, 'head', scatter_dimension=0, tiled=True)  75.3 us
    all_gather x1, waiting for transfers between devices, per_device(): lax.all_gather(arrived.reshape(experts * capacity, model_width), 'head',...  72.7 us
    pallas_call x1, Pallas kernels, attention_of(): pl.pallas_call(functools.partial(attend_kernel, tile=tile), grid_spec=plt...  61.5 us
    all_to_all x1, blocking collectives, per_device(): lax.all_to_all(outgoing, 'seq', split_axis=0, concat_axis=0, tiled=True)  46.1 us
    reduce_scatter x1, waiting for transfers between devices, per_device(): lax.psum_scatter(jnp.dot(attention, o_weight, preferred_element_type=jnp....  41.6 us
    all_to_all x1, waiting for transfers between devices, per_device(): lax.all_to_all(summed.reshape(experts, capacity, model_width), 'seq', spl...  37.4 us
    dot_general x1, matrix products, per_device(): jnp.dot(rows, w_gate_up[0].reshape(model_width, 2 * half), preferred_elem...  16.4 us
  transfers between devices with their start and end apart: 5, of which 4 were waited for; matrix products, arithmetic and copies ran while one was open for 3% of the time, Pallas kernels for 0%

profile of v1, /device:TPU:3, one launch (start us, length us, event | category | flops | bytes accessed | tf_op | source)
XLA Modules:
  0.0 430.9 jit_solution(996234523445910550)
XLA Ops:
  7.2 2.1 copy.56
  9.2 5.0 %all-to-all-start = ((bf16[8,64,640]{2,1,0:T(8,128)(2,1)}), bf16[8,64,640]{2,1,0:T(8,128)(2,1)S(1)}, u32[]{:S(2)}, u32[]{:S(2)}) async-start(bf16[8,64,640]{2,1,0:T(8,128)(2,1)} %bitcast.43), calls=%async_computation | async-start | bytes 1310720 | tf_op jit(solution)/shard_map/all_to_all | solution.py:135
  14.3 2.7 copy.55
  17.0 1.5 fusion.23
  18.5 3.6 pad_maximum_fusion.kk_ref
  22.8 3.4 concatenate.10.vv_ref
  27.0 61.5 %shard_map.113 = bf16[256,1024]{1,0:T(8,128)(2,1)} custom-call(s32[1]{0:T(128)S(6)} %copy.57.len_ref, bf16[4,2,64,640]{3,2,1,0:T(8,128)(2,1)} %bitcast.45, bf16[2,8192,128]{2,1,0:T(8,128)(2,1)} %pad_maximum_fusion.kk_ref, bf16[2,8192,128]{2,1,0:T(8,128)(2,1)} %concatenate.10.vv_ref), custom_call_target="tpu_custom_call" | custom-call | tf_op jit(solution)/shard_map/pallas_call | solution.py:89
  88.6 5.9 %convolution_convert_fusion.2 = bf16[256,2880]{1,0:T(8,128)(2,1)} fusion(bf16[256,1024]{1,0:T(8,128)(2,1)} %shard_map.113, bf16[1024,2880]{0,1:T(8,128)(2,1)} %param.14), kind=kOutput, calls=%fused_computation.5 | convolution fusion | flops 1510686720 | bytes 7897088 | tf_op jit(solution)/shard_map/dot_general | solution.py:145
  96.1 41.6 %reduce-scatter.3.cloned.1.call-done = bf16[64,2880]{1,0:T(8,128)(2,1)} async-done(((bf16[256,2880]{1,0:T(8,128)(2,1)}), bf16[64,2880]{1,0:T(8,128)(2,1)}) %reduce-scatter.3.cloned.1.call-update) | async-done | bytes 368656 | tf_op jit(solution)/shard_map/reduce_scatter | solution.py:144
  137.8 1.2 fusion.5
  139.0 3.0 convolution_convert_fusion.1
  142.0 2.7 reshape.66
  144.7 46.1 %all_to_all.15 = bf16[32,10,2880]{2,1,0:T(8,128)(2,1)} all-to-all(bf16[32,10,2880]{2,1,0:T(8,128)(2,1)S(1)} %reshape.66), channel_id=1, replica_groups=mesh['seq'=32,'head'=4] {'seq'}, dimensions={0} | all-to-all | bytes 3686400 | tf_op jit(solution)/shard_map/all_to_all | solution.py:177
  190.8 4.5 %reshape.67 = bf16[320,2880]{1,0:T(8,128)(2,1)} reshape(bf16[32,10,2880]{2,1,0:T(8,128)(2,1)} %all_to_all.15) | data formatting | bytes 3686400 | tf_op jit(solution)/shard_map/reshape | solution.py:179
  195.3 72.7 %all-gather.2.cloned.1.call-done = bf16[1280,2880]{1,0:T(8,128)(2,1)} async-done(((bf16[320,2880]{1,0:T(8,128)(2,1)}), bf16[1280,2880]{1,0:T(8,128)(2,1)}) %all-gather.2.cloned.1.call-update) | async-done | bytes 7372816 | tf_op jit(solution)/shard_map/all_gather | solution.py:178
  268.1 16.4 %fusion.24 = f32[1280,1440]{0,1:T(8,128)S(1)} fusion(bf16[1280,2880]{1,0:T(8,128)(2,1)} %all-gather.2.cloned.1.call-done, bf16[2880,1440]{0,1:T(8,128)(2,1)} %bitcast.46), kind=kOutput, calls=%fused_computation.44 | convolution fusion | flops 10616832000 | bytes 23040000 | tf_op jit(solution)/shard_map/dot_general | solution.py:181
  284.5 8.5 %convolution_convert_fusion = bf16[1280,2880]{1,0:T(8,128)(2,1)} fusion(bf16[1,720,2880]{2,1,0:T(8,128)(2,1)S(1)} %bitcast.48, f32[1280,1440]{0,1:T(8,128)S(1)} %fusion.24), kind=kOutput, calls=%fused_computation | convolution fusion | flops 5317632000 | bytes 18892800 | tf_op jit(solution)/shard_map/dot_general | solution.py:187
  293.0 75.3 %reduce-scatter.5.cloned.1.call-done = bf16[320,2880]{1,0:T(8,128)(2,1)} async-done(((bf16[1280,2880]{1,0:T(8,128)(2,1)}), bf16[320,2880]{1,0:T(8,128)(2,1)}) %reduce-scatter.5.cloned.1.call-update) | async-done | bytes 1843216 | tf_op jit(solution)/shard_map/reduce_scatter | solution.py:188
  368.3 4.2 reshape.68
  372.5 7.9 %all-to-all-start.2 = ((bf16[32,10,2880]{2,1,0:T(8,128)(2,1)}), bf16[32,10,2880]{2,1,0:T(8,128)(2,1)S(1)}, u32[]{:S(2)}, u32[]{:S(2)}) async-start(bf16[32,10,2880]{2,1,0:T(8,128)(2,1)} %reshape.68), calls=%async_computation.4 | async-start | bytes 6029312 | tf_op jit(solution)/shard_map/all_to_all | solution.py:189
  380.6 37.4 %all-to-all-done.2 = bf16[32,10,2880]{2,1,0:T(8,128)(2,1)S(1)} async-done(((bf16[32,10,2880]{2,1,0:T(8,128)(2,1)}), bf16[32,10,2880]{2,1,0:T(8,128)(2,1)S(1)}, u32[]{:S(2)}, u32[]{:S(2)}) %all-to-all-start.2) | async-done | bytes 1843232 | tf_op jit(solution)/shard_map/all_to_all | solution.py:189
  418.0 2.4 reshape.69
  420.4 2.5 fusion.12
  423.4 1.0 copy.50
  (39 shorter events, 3.2 us)
Async XLA Ops:
  9.2 16.9 %all-to-all-start = ((bf16[8,64,640]{2,1,0:T(8,128)(2,1)}), bf16[8,64,640]{2,1,0:T(8,128)(2,1)S(1)}, u32[]{:S(2)}, u32[]{:S(2)}) async-start(bf16[8,64,640]{2,1,0:T(8,128)(2,1)} %bitcast.43), calls=%async_computation | async-start | bytes 1310720 | tf_op jit(solution)/shard_map/all_to_all | solution.py:135
  14.3 123.5 %reduce-scatter.3.cloned.1.call-start = ((), (), s32[]{:S(2)}) async-start(), calls=%async_computation.5 | async-start | bytes 1884160 | tf_op jit(solution)/shard_map/reduce_scatter | solution.py:144
  26.1 0.9 copy-start
  88.6 6.0 %copy-start.3 = (s32[64,4]{0,1:T(4,128)S(1)}, s32[64,4]{0,1:T(4,128)}, u32[]{:S(2)}) copy-start(s32[64,4]{0,1:T(4,128)} %param.16) | copy-start | bytes 3076
  88.6 49.2 %copy-start.1 = (bf16[64,2880]{1,0:T(8,128)(2,1)S(1)}, bf16[64,2880]{1,0:T(8,128)(2,1)}, u32[]{:S(2)}) copy-start(bf16[64,2880]{1,0:T(8,128)(2,1)} %param.10) | copy-start | bytes 1105924
  88.6 50.4 %copy-start.2 = (f32[2880]{0:T(1024)S(1)}, f32[2880]{0:T(1024)}, u32[]{:S(2)}) copy-start(f32[2880]{0:T(1024)} %param.15) | copy-start | bytes 34564
  94.5 173.6 %all-gather.2.cloned.1.call-start = ((), (), s32[]{:S(2)}) async-start(), calls=%async_computation.6 | async-start | bytes 9420800 | tf_op jit(solution)/shard_map/all_gather | solution.py:178
  195.3 89.2 %slice-start = ((s8[4239360]{0:T(1024)(128)(4,1)}), s8[45056]{0:T(1024)(128)(4,1)S(1)}, s32[]{:S(2)}) async-start(s8[4239360]{0:T(1024)(128)(4,1)} %bitcast.47), calls=%async_computation.8 | async-start | bytes 90112
  195.3 173.1 %reduce-scatter.5.cloned.1.call-start = ((), (), s32[]{:S(2)}) async-start(), calls=%async_computation.7 | async-start | bytes 9420800 | tf_op jit(solution)/shard_map/reduce_scatter | solution.py:188
  268.1 16.4 %slice-start.1 = ((s8[4239360]{0:T(1024)(128)(4,1)}), s8[4194304]{0:T(1024)(128)(4,1)S(1)}, s32[]{:S(2)}) async-start(s8[4239360]{0:T(1024)(128)(4,1)} %bitcast.47), calls=%async_computation.9 | async-start | bytes 8388608
  372.5 7.9 %copy-start.4 = (f32[64,4]{0,1:T(4,128)S(1)}, f32[64,4]{0,1:T(4,128)}, u32[]{:S(2)}) copy-start(f32[64,4]{0,1:T(4,128)} %param.17) | copy-start | bytes 3076
  372.5 45.5 %all-to-all-start.2 = ((bf16[32,10,2880]{2,1,0:T(8,128)(2,1)}), bf16[32,10,2880]{2,1,0:T(8,128)(2,1)S(1)}, u32[]{:S(2)}, u32[]{:S(2)}) async-start(bf16[32,10,2880]{2,1,0:T(8,128)(2,1)} %reshape.68), calls=%async_computation.4 | async-start | bytes 6029312 | tf_op jit(solution)/shard_map/all_to_all | solution.py:189
Sparse Core Ops, SparseCore 0:
  94.6 43.1 reduce-scatter.2
  195.4 72.6 all-gather.1
  293.2 75.1 reduce-scatter.4
